TPU v7x, 32 devices: a whole 2x2x4 slice. The times are simulated.
32 devices in a mesh: grp: 8 (over y, x, core), seq: 4 (over z).
Axes of the slice: x: 2, y: 2, z: 4, core: 2. Of those that a mesh axis runs over, the one named last changes fastest.
Arguments:
- tokens: bfloat16 [8192, 512], P(('grp', 'seq')), parts along dimension 0, may hold values from -6 to 6
- group_pos: int32 [2048], P('grp'), parts along dimension 0, may hold values from 0 to 1023, as said below
- log_decay: float32 [8192, 16], P(('grp', 'seq')), parts along dimension 0, may hold values from -1 to 0, as said below
- in_weight: bfloat16 [512, 2176], replicated, may hold values from -0.25 to 0.25
- norm_gain: float32 [1024], replicated, may hold values from 0.1 to 1.9
- out_weight: bfloat16 [1024, 512], replicated, may hold values from -0.1875 to 0.1875
- inner_gain: float32 [512], replicated, may hold values from 0.1 to 1.9
- qkv_weight: bfloat16 [4, 512, 192], P('seq'), may hold values from -1 to 1
- attn_out: bfloat16 [4, 64, 512], P('seq'), may hold values from -0.375 to 0.375
Outputs:
- result: bfloat16 [8192, 512], P(('grp', 'seq')), parts along dimension 0
There are 8 independent parts, one for each index of `grp`. A program takes and returns all parts, laid end to end along the dimension named above; an argument that names none is the same for every part. Nothing has to cross between parts.
Inputs may be any that keep to these rules, and one draw needn't show every extreme that they name: `group_pos`: strictly increasing. Each device's 256 positions hold at least one group start and at most 128; some device holds exactly 128. `log_decay`: negative at every position.
All inputs are finite; a program needn't handle non-finite values.
Results may differ from a plain program's by a relative error of at most 0.0061.
Values may be sent and summed in bfloat16 or wider, within the bound.
No kernel may reach another device: no remote copies, remote signals or barrier semaphores. Data moves between devices by JAX's collectives and lax.ppermute only.
A program may use at most 64 MiB of HBM per device.

v0:
```python
import jax
import jax.numpy as jnp
from jax import lax
from jax.sharding import PartitionSpec as P


def entering(value, axis, join, neutral):
    count, mine = (lax.axis_size(axis), lax.axis_index(axis))
    pieces = jax.tree.map(lambda part: lax.all_gather(part, axis), value)
    subtotal = jax.tree.map(
        lambda part, zero: jnp.full_like(part, 0) + jnp.asarray(zero, part.dtype), value, neutral
    )

    def turn(position, subtotal):
        longer = join(subtotal, jax.tree.map(lambda part: part[position], pieces))
        return jax.tree.map(lambda new, old: jnp.where(position < mine, new, old), longer, subtotal)

    return lax.fori_loop(0, count - 1, turn, subtotal)


def rms_norm(values, gain):
    return values * lax.rsqrt(jnp.mean(values * values, axis=-1, keepdims=True) + 1e-05) * gain


def attend(rows, w_qkv, index, valid):
    head_dim = w_qkv.shape[1] // 3
    qkv = jnp.dot(rows, w_qkv, preferred_element_type=jnp.float32).astype(jnp.bfloat16)
    query = qkv[:, :head_dim]
    keys = qkv[:, head_dim : 2 * head_dim]
    values = qkv[:, 2 * head_dim :]
    count = rows.shape[0]
    block = min(512, count)

    def one_block(start):
        query_block = lax.dynamic_slice_in_dim(query, start, block, 0)
        index_block = lax.dynamic_slice_in_dim(index, start, block, 0)
        scores = jnp.dot(query_block, keys.T, preferred_element_type=jnp.float32) * head_dim ** (
            -0.5
        )
        allowed = (index[None, :] <= index_block[:, None]) & valid[None, :]
        scores = jnp.where(allowed, scores, -jnp.inf)
        top = jnp.max(scores, axis=1, keepdims=True)
        expo = jnp.exp(scores - top)
        probs = (expo / jnp.sum(expo, axis=1, keepdims=True)).astype(jnp.bfloat16)
        return jnp.dot(probs, values, preferred_element_type=jnp.float32).astype(jnp.bfloat16)

    starts = jnp.arange(count // block, dtype=jnp.int32) * block
    return lax.map(one_block, starts).reshape(count, head_dim)


def shards(
    tokens, group_pos, log_decay, in_weight, norm_gain, out_weight, inner_gain, qkv_weight, attn_out
):
    highest = lax.Precision.HIGHEST
    length = tokens.shape[0]
    heads = log_decay.shape[1]
    width = out_weight.shape[0]
    model_width = out_weight.shape[1]
    head_size = width // heads
    state_dim = (in_weight.shape[1] - 2 * width) // 2
    proj = jnp.dot(tokens, in_weight, preferred_element_type=jnp.float32).astype(jnp.bfloat16)
    xs = proj[:, :width].astype(jnp.float32).reshape(length, heads, head_size)
    gate = proj[:, width : 2 * width].astype(jnp.float32)
    bmat = proj[:, 2 * width : 2 * width + state_dim].astype(jnp.float32)
    cmat = proj[:, 2 * width + state_dim :].astype(jnp.float32)
    cumul = jnp.cumsum(log_decay, axis=0)
    differ = cumul.T[:, :, None] - cumul.T[:, None, :]
    lower = jnp.arange(length)[:, None] >= jnp.arange(length)[None, :]
    decays = jnp.exp(jnp.where(lower[None], differ, -jnp.inf))
    intersections = jnp.dot(cmat, bmat.T, precision=highest)
    within = jnp.einsum("hij,jhp->ihp", decays * intersections[None], xs, precision=highest)
    tails = jnp.exp(cumul[-1][None, :] - cumul)
    local_state = jnp.einsum("jh,jhp,jn->hpn", tails, xs, bmat, precision=highest)
    total_decay = jnp.exp(cumul[-1])

    def link(earlier, later):
        return (earlier[0] * later[0], later[0][:, None, None] * earlier[1] + later[1])

    identity = (jnp.ones_like(total_decay), jnp.zeros_like(local_state))
    _, state_in = entering((total_decay, local_state), "seq", link, identity)
    carried = jnp.einsum("ih,in,hpn->ihp", jnp.exp(cumul), cmat, state_in, precision=highest)
    gated = (within + carried).reshape(length, width) * jax.nn.silu(gate)
    normed = rms_norm(gated, norm_gain).astype(jnp.bfloat16)
    hidden = (
        tokens.astype(jnp.float32) + jnp.dot(normed, out_weight, preferred_element_type=jnp.float32)
    ).astype(jnp.bfloat16)
    position = lax.axis_index("seq")
    devices = lax.axis_size("seq")
    most = length // 2
    groups = group_pos.shape[0]
    starts = jnp.arange(devices, dtype=jnp.int32) * length
    before = jnp.sum((group_pos[None, :] < starts[:, None]).astype(jnp.int32), axis=1)
    upto = jnp.sum((group_pos[None, :] < (starts + length)[:, None]).astype(jnp.int32), axis=1)
    counts = upto - before
    slots = jnp.arange(most, dtype=jnp.int32)
    picks = jnp.clip(before[position] + slots, 0, groups - 1)
    valid_here = slots < counts[position]
    local_pos = group_pos[picks] - position * length
    placing = (
        (local_pos[:, None] == jnp.arange(length, dtype=jnp.int32)[None, :]) & valid_here[:, None]
    ).astype(jnp.float32)
    rows = jnp.dot(placing.astype(jnp.bfloat16), hidden, preferred_element_type=jnp.float32)
    rows_n = rms_norm(rows, inner_gain).astype(jnp.bfloat16)
    gathered = lax.all_gather(rows_n, "seq", axis=0, tiled=True)
    slot_group = (before[:, None] + slots[None, :]).reshape(-1)
    slot_valid = (slots[None, :] < counts[:, None]).reshape(-1)
    w_qkv = qkv_weight[0]
    heads_out = attend(gathered, w_qkv, slot_group, slot_valid)
    full_out = lax.all_gather(attn_out, "seq", axis=0, tiled=True)
    mine = lax.all_to_all(heads_out[:, None, :], "seq", split_axis=0, concat_axis=1, tiled=True)
    back = jnp.dot(
        mine.reshape(most, -1),
        full_out.reshape(-1, model_width),
        preferred_element_type=jnp.float32,
    )
    placed = jnp.dot(placing.T, back, precision=highest)
    return (hidden.astype(jnp.float32) + placed).astype(jnp.bfloat16)


def solution(mesh):
    in_specs = (
        P(("grp", "seq"), None),
        P("grp"),
        P(("grp", "seq"), None),
        P(),
        P(),
        P(),
        P(),
        P("seq", None, None),
        P("seq", None, None),
    )
    out_specs = P(("grp", "seq"), None)
    return jax.shard_map(shards, mesh=mesh, in_specs=in_specs, out_specs=out_specs, check_vma=False)
```

profile of v0, /device:TPU:0, one launch (start us, length us, event | category | flops | bytes accessed | tf_op | source)
XLA Modules:
  0.0 115.9 jit_solution(2016591434502746078)
XLA Ops:
  6.5 0.9 copy_bitcast_fusion.1
  7.4 0.6 reduce-window.6
  8.6 1.9 %convolution_convert_fusion = bf16[256,2176]{0,1:T(8,128)(2,1)S(1)} fusion(bf16[256,512]{1,0:T(8,128)(2,1)} %param.11, bf16[512,2176]{1,0:T(8,128)(2,1)S(1)} %copy-done), kind=kOutput, calls=%fused_computation.9 | convolution fusion | flops 570982400 | bytes 3604480 | tf_op jit(solution)/shard_map/dot_general | solution.py:61
  10.6 1.0 copy-done.2
  11.5 1.5 %fusion.23 = f32[16,64,64]{2,1,0:T(8,128)} fusion(bf16[256,16,64]{0,2,1:T(8,128)(2,1)S(1)} %bitcast.77, f32[256,16]{0,1:T(8,128)S(1)} %get-tuple-element.159, bf16[256,2176]{0,1:T(8,128)(2,1)S(1)} %convolution_convert_fusion), kind=kOutput, calls=%fused_computation.37 | convolution fusion | flops 201850880 | bytes 835584 | tf_op jit(solution)/shard_map/jh,jhp,jn->hpn/dot_general | solution.py:73
  13.2 0.6 dynamic_slice.27
  13.8 0.7 fusion.50
  14.5 0.6 dynamic_slice.28
  15.1 0.6 iota_compare_fusion.3
  15.8 1.3 %gather_fusion = s32[128]{0:T(128)S(1)} fusion(s32[256]{0:T(256)S(1)} %copy-done.1, s32[1024]{0:T(1024)S(1)} %pad_clamp_fusion), kind=kCustom, calls=%fused_computation | custom fusion | bytes 1536 | tf_op jit(solution)/shard_map/gather | solution.py:98
  17.1 12.7 %all-gather.1 = f32[4,1,16]{2,1,0:T(1,128)S(1)} all-gather(f32[1,1,16]{2,1,0:T(1,128)S(1)} %bitcast.82), channel_id=1, replica_groups=mesh['grp'=8,'seq'=4] {'seq'}, dimensions={0}, use_global_device_ids=true | all-gather | bytes 320 | tf_op jit(solution)/shard_map/all_gather | solution.py:9
  29.9 0.8 slice_convert_fusion
  30.7 1.0 fusion.46
  31.7 4.1 %fusion.11 = f32[256,16,64]{0,2,1:T(8,128)} fusion(bf16[256,16,64]{0,2,1:T(8,128)(2,1)S(1)} %bitcast.78, f32[256,256]{1,0:T(8,128)S(1)} %fusion.46, f32[16,256]{1,0:T(8,128)S(1)} %get-tuple-element.161, pred[256,256]{1,0:T(8,128)(4,1)S(1)} %iota_compare_fusion), kind=kOutput, calls=%fused_computation.15 | convolution fusion | flops 808452096 | bytes 1916928 | tf_op jit(solution)/shard_map/hij,jhp->ihp/dot_general | solution.py:71
  35.7 25.8 %all-gather.4.cloned.1.call-done = f32[64,64,64]{2,1,0:T(8,128)} async-done(((f32[16,64,64]{2,1,0:T(8,128)}), f32[64,64,64]{2,1,0:T(8,128)}) %all-gather.4.cloned.1.call-update) | async-done | bytes 1048592 | tf_op jit(solution)/shard_map/all_gather | solution.py:9
  61.6 3.6 %while.18 = (s32[]{:T(128)}, f32[16,64,64]{2,1,0:T(8,128)S(1)}, s32[]{:T(128)}, f32[4,16]{1,0:T(4,128)S(1)}, f32[4,16,64,64]{3,2,1,0:T(8,128)}, /*index=5*/s32[]{:T(128)}, s32[]{:T(128)}) while((s32[]{:T(128)}, f32[16,64,64]{2,1,0:T(8,128)S(1)}, s32[]{:T(128)}, f32[4,16]{1,0:T(4,128)S(1)}, f32[4,16,64,64]{3,2,1,0:T(8,128)}, ...), condition=%wide.region_3.4_spmd.clone, body=%wide.region_2.3_spmd.clone.sunk | while | flops 262148 | bytes 786729 | solution.py:18
  61.6 1.2 %fusion.68 = f32[16,64,64]{2,1,0:T(8,128)S(1)} fusion(f32[4,16,64,64]{3,2,1,0:T(8,128)} %get-tuple-element.217, s32[]{:T(128)} %get-tuple-element.206, f32[16,64,64]{2,1,0:T(8,128)S(1)} %get-tuple-element.207, f32[16]{0:T(128)S(1)} %dynamic-slice_bitcast_fusion.2, pred[]{:T(512)S(6)} %compare.3, pred[]{:T(512)S(6)} %lt.120), kind=kLoop, calls=%fused_computation.2.clone.1 | loop fusion | flops 262144 | bytes 786502 | tf_op jit(solution)/shard_map/while/body/eval_jaxpr/jit(_where)/select_n | solution.py:16
  62.8 1.2 %fusion.68 = f32[16,64,64]{2,1,0:T(8,128)S(1)} fusion(f32[4,16,64,64]{3,2,1,0:T(8,128)} %get-tuple-element.217, s32[]{:T(128)} %get-tuple-element.206, f32[16,64,64]{2,1,0:T(8,128)S(1)} %get-tuple-element.207, f32[16]{0:T(128)S(1)} %dynamic-slice_bitcast_fusion.2, pred[]{:T(512)S(6)} %compare.3, pred[]{:T(512)S(6)} %lt.120), kind=kLoop, calls=%fused_computation.2.clone.1 | loop fusion | flops 262144 | bytes 786502 | tf_op jit(solution)/shard_map/while/body/eval_jaxpr/jit(_where)/select_n | solution.py:16
  64.0 1.2 %fusion.68 = f32[16,64,64]{2,1,0:T(8,128)S(1)} fusion(f32[4,16,64,64]{3,2,1,0:T(8,128)} %get-tuple-element.217, s32[]{:T(128)} %get-tuple-element.206, f32[16,64,64]{2,1,0:T(8,128)S(1)} %get-tuple-element.207, f32[16]{0:T(128)S(1)} %dynamic-slice_bitcast_fusion.2, pred[]{:T(512)S(6)} %compare.3, pred[]{:T(512)S(6)} %lt.120), kind=kLoop, calls=%fused_computation.2.clone.1 | loop fusion | flops 262144 | bytes 786502 | tf_op jit(solution)/shard_map/while/body/eval_jaxpr/jit(_where)/select_n | solution.py:16
  65.2 2.4 %fusion.15 = f32[256,16,64]{0,2,1:T(8,128)S(1)} fusion(f32[256,16,64]{0,2,1:T(8,128)} %fusion.11, f32[16,64,64]{2,1,0:T(8,128)S(1)} %get-tuple-element.123, f32[256,16]{0,1:T(8,128)S(1)} %get-tuple-element.158, f32[256,64]{0,1:T(8,128)S(1)} %slice_convert_fusion), kind=kOutput, calls=%fused_computation.19 | convolution fusion | flops 201850880 | bytes 2441216 | tf_op jit(solution)/shard_map/ih,in,hpn->ihp/dot_general | solution.py:81
  67.6 1.4 %multiply_reduce_fusion = (f32[256]{0:T(256)S(1)}, f32[256,1024]{0,1:T(8,128)S(1)}) fusion(bf16[256,2176]{0,1:T(8,128)(2,1)} %copy-done.2, f32[256,16,64]{0,2,1:T(8,128)S(1)} %fusion.15), kind=kLoop, calls=%fused_computation.36 | loop fusion | flops 2096896 | bytes 2622464 | tf_op jit(solution)/shard_map/reduce_sum | solution.py:22
  69.1 0.8 fusion.16
  69.9 0.3 multiply_reduce_fusion.1
  70.3 15.6 %all_gather.19 = bf16[512,512]{1,0:T(8,128)(2,1)S(1)} all-gather(bf16[128,512]{1,0:T(8,128)(2,1)S(1)} %multiply_convert_fusion.2), channel_id=1, replica_groups=mesh['grp'=8,'seq'=4] {'seq'}, dimensions={0}, use_global_device_ids=true | all-gather | bytes 655360 | tf_op jit(solution)/shard_map/all_gather | solution.py:104
  85.9 0.3 convolution_convert_fusion.1
  86.3 0.5 fusion.54
  87.2 0.5 broadcast.142
  87.8 0.7 reduce.6
  88.6 0.8 reshape.183
  89.4 3.3 %all-to-all-start = ((bf16[4,2,4096]{2,1,0:T(2,128)(2,1)}), bf16[4,2,4096]{2,1,0:T(2,128)(2,1)S(1)}, u32[]{:S(2)}, u32[]{:S(2)}) async-start(bf16[4,2,4096]{2,1,0:T(2,128)(2,1)} %reshape.183), calls=%async_computation | async-start | bytes 131072 | tf_op jit(solution)/shard_map/all_to_all | solution.py:110
  92.7 14.6 %all_gather.20 = bf16[4,64,512]{2,1,0:T(8,128)(2,1)S(1)} all-gather(bf16[1,64,512]{2,1,0:T(8,128)(2,1)S(1)} %copy-done.6), channel_id=1, replica_groups=mesh['grp'=8,'seq'=4] {'seq'}, dimensions={0}, use_global_device_ids=true | all-gather | bytes 327680 | tf_op jit(solution)/shard_map/all_gather | solution.py:109
  107.8 1.2 %fusion.17 = bf16[256,512]{1,0:T(8,128)(2,1)} fusion(f32[128,512]{1,0:T(8,128)S(1)} %fusion.55, bf16[256,512]{1,0:T(8,128)(2,1)S(1)} %fusion.16, s32[128]{0:T(128)S(1)} %broadcast_subtract_fusion, pred[128]{0:T(512)(128)(4,1)S(1)} %iota_compare_fusion.3), kind=kOutput, calls=%fused_computation.25 | convolution fusion | flops 201785344 | bytes 787072 | tf_op jit(solution)/shard_map/dot_general | solution.py:116
  (50 shorter events, 2.3 us)
Async XLA Ops:
  6.5 2.0 %copy-start = (bf16[512,2176]{1,0:T(8,128)(2,1)S(1)}, bf16[512,2176]{1,0:T(8,128)(2,1)}, u32[]{:S(2)}) copy-start(bf16[512,2176]{1,0:T(8,128)(2,1)} %param.14) | copy-start | bytes 6684676
  6.5 55.0 %all-gather.4.cloned.1.call-start = ((), (), s32[]{:S(2)}) async-start(), calls=%async_computation.1 | async-start | bytes 2621440 | tf_op jit(solution)/shard_map/all_gather | solution.py:9
  10.5 1.0 copy-start.2
  10.5 2.5 %copy-start.1 = (s32[256]{0:T(256)S(1)}, s32[256]{0:T(256)}, u32[]{:S(2)}) copy-start(s32[256]{0:T(256)} %param.12) | copy-start | bytes 3076
  65.2 3.9 %copy-start.3 = (bf16[256,512]{1,0:T(8,128)(2,1)S(1)}, bf16[256,512]{1,0:T(8,128)(2,1)}, u32[]{:S(2)}) copy-start(bf16[256,512]{1,0:T(8,128)(2,1)} %param.11) | copy-start | bytes 786436
  65.2 3.9 %copy-start.4 = (bf16[1024,512]{1,0:T(8,128)(2,1)S(1)}, bf16[1024,512]{1,0:T(8,128)(2,1)}, u32[]{:S(2)}) copy-start(bf16[1024,512]{1,0:T(8,128)(2,1)} %param.16) | copy-start | bytes 3145732
  65.2 3.9 %copy-start.7 = (f32[1024]{0:T(1024)S(1)}, f32[1024]{0:T(1024)}, u32[]{:S(2)}) copy-start(f32[1024]{0:T(1024)} %param.15) | copy-start | bytes 12292
  69.0 1.2 %copy-start.8 = (f32[512]{0:T(512)S(1)}, f32[512]{0:T(512)}, u32[]{:S(2)}) copy-start(f32[512]{0:T(512)} %param.17) | copy-start | bytes 6148
  69.0 16.9 %copy-start.5 = (bf16[1,512,192]{1,2,0:T(8,128)(2,1)S(1)}, bf16[1,512,192]{1,2,0:T(8,128)(2,1)}, u32[]{:S(2)}) copy-start(bf16[1,512,192]{1,2,0:T(8,128)(2,1)} %param.18) | copy-start | bytes 589828
  86.9 5.7 %copy-start.6 = (bf16[1,64,512]{2,1,0:T(8,128)(2,1)S(1)}, bf16[1,64,512]{2,1,0:T(8,128)(2,1)}, u32[]{:S(2)}) copy-start(bf16[1,64,512]{2,1,0:T(8,128)(2,1)} %param.19) | copy-start | bytes 196612
  89.4 17.9 %all-to-all-start = ((bf16[4,2,4096]{2,1,0:T(2,128)(2,1)}), bf16[4,2,4096]{2,1,0:T(2,128)(2,1)S(1)}, u32[]{:S(2)}, u32[]{:S(2)}) async-start(bf16[4,2,4096]{2,1,0:T(2,128)(2,1)} %reshape.183), calls=%async_computation | async-start | bytes 131072 | tf_op jit(solution)/shard_map/all_to_all | solution.py:110
Sparse Core Ops, SparseCore 0:
  13.1 48.3 all-gather.3
where the time goes:
time: 117 us; the launch traced here: 116 us
  blocking collectives  42.9 us (37%)
  waiting for transfers between devices  25.9 us (22%)
  matrix products  14.4 us (12%)
  between operations  13.7 us (12%)
  other arithmetic  9.12 us (8%)
  local copies, waits for them, and re-layouts  6.46 us (6%)
  starting transfers between devices  3.29 us (3%)
    all_gather x1, waiting for transfers between devices, entering(): pieces = jax.tree.map(lambda part: lax.all_gather(part, axis), value)  25.8 us
    all_gather x1, blocking collectives, shards(): gathered = lax.all_gather(rows_n, 'seq', axis=0, tiled=True)  15.6 us
    all_gather x1, blocking collectives, shards(): full_out = lax.all_gather(attn_out, 'seq', axis=0, tiled=True)  14.6 us
    all_gather x1, blocking collectives, entering(): pieces = jax.tree.map(lambda part: lax.all_gather(part, axis), value)  12.7 us
    dot_general x1, matrix products, shards(): jnp.einsum('hij,jhp->ihp', decays * intersections[None], xs, precision=hi...  4.07 us
    select_n x3, other arithmetic, turn(): jnp.where(position < mine, new, old)  3.51 us
    all_to_all x1, starting transfers between devices, shards(): lax.all_to_all(heads_out[:, None, :], 'seq', split_axis=0, concat_axis=1,...  3.28 us
    dot_general x1, matrix products, shards(): jnp.einsum('ih,in,hpn->ihp', jnp.exp(cumul), cmat, state_in, precision=hi...  2.42 us
  transfers between devices with their start and end apart: 2, of which 1 were waited for; matrix products, arithmetic and copies ran while one was open for 9% of the time, Pallas kernels for 0%

commit v1 on v0

--- a/solution.py
+++ b/solution.py
@@ -106,7 +106,12 @@
     slot_valid = (slots[None, :] < counts[:, None]).reshape(-1)
     w_qkv = qkv_weight[0]
     heads_out = attend(gathered, w_qkv, slot_group, slot_valid)
-    full_out = lax.all_gather(attn_out, "seq", axis=0, tiled=True)
+    ring = [attn_out]
+    for hop in range(3):
+        ring.append(lax.ppermute(ring[-1], "seq", [(dev, (dev + 1) % 4) for dev in range(4)]))
+    full_out = jnp.roll(
+        jnp.concatenate(ring[::-1], axis=0), (lax.axis_index("seq") + 1) * ring[0].shape[0], axis=0
+    )
     mine = lax.all_to_all(heads_out[:, None, :], "seq", split_axis=0, concat_axis=1, tiled=True)
     back = jnp.dot(
         mine.reshape(most, -1),

time: 117 us -> 111 us (0.949)
  blocking collectives: 42.9 us -> 25.8 us
  local copies, waits for them, and re-layouts: 6.46 us -> 13.1 us
  starting transfers between devices: 3.29 us -> 8.02 us
  waiting for transfers between devices: 25.9 us -> 21.9 us
  other arithmetic: 9.12 us -> 12.5 us
  matrix products: 14.4 us -> 15.8 us
    all_gather x1, waiting for transfers between devices: 25.8 us -> 10.3 us  [entering(): pieces = jax.tree.map(lambda part: lax.all_gather(part, axis), value)]
    all_gather x1 -> x0, blocking collectives: 14.6 us -> none  [shards(): full_out = lax.all_gather(attn_out, 'seq', axis=0, tiled=True)]
    ppermute x0 -> x3, waiting for transfers between devices: none -> 6.9 us  [shards(): lax.ppermute(ring[-1], 'seq', [(dev, (dev + 1) % 4) for dev in range(4)])]
    ppermute x0 -> x3, starting transfers between devices: none -> 4.74 us  [shards(): lax.ppermute(ring[-1], 'seq', [(dev, (dev + 1) % 4) for dev in range(4)])]
    all_to_all x1, waiting for transfers between devices: 0.01 us -> 4.73 us  [shards(): lax.all_to_all(heads_out[:, None, :], 'seq', split_axis=0, concat_axis=1,...]
    unnamed x21 -> x34, local copies, waits for them, and re-layouts: 2.07 us -> 6.28 us
    all_gather x1, blocking collectives: 12.7 us -> 10.2 us  [entering(): pieces = jax.tree.map(lambda part: lax.all_gather(part, axis), value)]
    dot_general x1, matrix products: 4.07 us -> 5.45 us  [shards(): jnp.einsum('hij,jhp->ihp', decays * intersections[None], xs, precision=hi...]
  transfers between devices with their start and end apart: 2 -> 5, of which waited for: 1 -> 3; matrix products, arithmetic and copies ran while one was open for 9% -> 18% of each run, Pallas kernels for 0% -> 0%
where the time goes in v1:
time: 111 us
  blocking collectives  25.8 us (23%)
  waiting for transfers between devices  21.9 us (20%)
  matrix products  15.8 us (14%)
  between operations  13.7 us (12%)
  local copies, waits for them, and re-layouts  13.1 us (12%)
  other arithmetic  12.5 us (11%)
  starting transfers between devices  8.02 us (7%)
    all_gather x1, blocking collectives, shards(): gathered = lax.all_gather(rows_n, 'seq', axis=0, tiled=True)  15.6 us
    all_gather x1, waiting for transfers between devices, entering(): pieces = jax.tree.map(lambda part: lax.all_gather(part, axis), value)  10.3 us
    all_gather x1, blocking collectives, entering(): pieces = jax.tree.map(lambda part: lax.all_gather(part, axis), value)  10.2 us
    ppermute x3, waiting for transfers between devices, shards(): lax.ppermute(ring[-1], 'seq', [(dev, (dev + 1) % 4) for dev in range(4)])  6.9 us
    unnamed x34, local copies, waits for them, and re-layouts  6.28 us
    dot_general x1, matrix products, shards(): jnp.einsum('hij,jhp->ihp', decays * intersections[None], xs, precision=hi...  5.45 us
    ppermute x3, starting transfers between devices, shards(): lax.ppermute(ring[-1], 'seq', [(dev, (dev + 1) % 4) for dev in range(4)])  4.74 us
    all_to_all x1, waiting for transfers between devices, shards(): lax.all_to_all(heads_out[:, None, :], 'seq', split_axis=0, concat_axis=1,...  4.73 us
  transfers between devices with their start and end apart: 5, of which 3 were waited for; matrix products, arithmetic and copies ran while one was open for 18% of the time, Pallas kernels for 0%

profile of v1, /device:TPU:0, one launch (start us, length us, event | category | flops | bytes accessed | tf_op | source)
XLA Modules:
  0.0 110.8 jit_solution(1094712291167799552)
XLA Ops:
  6.5 0.9 copy_bitcast_fusion.1
  8.2 0.7 fusion.52
  9.0 0.7 bitcast_exponential_fusion
  9.7 1.9 %convolution_convert_fusion = bf16[256,2176]{0,1:T(8,128)(2,1)S(1)} fusion(bf16[256,512]{1,0:T(8,128)(2,1)} %param.11, bf16[512,2176]{1,0:T(8,128)(2,1)S(1)} %copy-done), kind=kOutput, calls=%fused_computation.9 | convolution fusion | flops 570982400 | bytes 3604480 | tf_op jit(solution)/shard_map/dot_general | solution.py:61
  11.8 0.8 copy-done.3
  12.6 1.5 %fusion.23 = f32[16,64,64]{2,1,0:T(8,128)} fusion(bf16[256,16,64]{0,2,1:T(8,128)(2,1)S(1)} %bitcast.77, f32[256,16]{0,1:T(8,128)S(1)} %get-tuple-element.159, bf16[256,2176]{0,1:T(8,128)(2,1)S(1)} %convolution_convert_fusion), kind=kOutput, calls=%fused_computation.37 | convolution fusion | flops 201850880 | bytes 835584 | tf_op jit(solution)/shard_map/jh,jhp,jn->hpn/dot_general | solution.py:73
  14.1 3.1 %collective-permute-start = (bf16[1,64,512]{2,1,0:T(8,128)(2,1)S(1)}, bf16[1,64,512]{2,1,0:T(8,128)(2,1)S(1)}, u32[]{:S(2)}, u32[]{:S(2)}) collective-permute-start(bf16[1,64,512]{2,1,0:T(8,128)(2,1)S(1)} %copy-done.6), channel_id=1, source_target_pairs={{0,1},{1,2},{2,3},{3,0},{4,5},{5,6},{6,7},{7,4},{8,9},{9,10},{10,1... | collective-permute-start | bytes 196616 | tf_op jit(solution)/shard_map/ppermute | solution.py:111
  17.2 0.9 fusion.46
  19.3 1.3 %convert_reduce_fusion = (s32[4]{0:T(128)}, s32[4]{0:T(128)S(1)}) fusion(s32[256]{0:T(256)S(1)} %copy-done.1, s32[4]{0:T(128)} %get-tuple-element.167, s32[4]{0:T(128)S(1)} %get-tuple-element.166), kind=kLoop, calls=%fused_computation.84 | loop fusion | flops 6136 | bytes 1088 | tf_op jit(solution)/shard_map/reduce_sum | solution.py:93
  21.3 0.7 fusion.50
  22.6 5.5 %fusion.11 = f32[256,16,64]{0,2,1:T(8,128)} fusion(bf16[256,16,64]{0,2,1:T(8,128)(2,1)} %bitcast.78, f32[256,256]{1,0:T(8,128)} %fusion.46, f32[16,256]{1,0:T(8,128)} %get-tuple-element.161, pred[256,256]{1,0:T(8,128)(4,1)} %iota_compare_fusion), kind=kOutput, calls=%fused_computation.15 | convolution fusion | flops 808452096 | bytes 1916928 | tf_op jit(solution)/shard_map/hij,jhp->ihp/dot_general | solution.py:71
  28.1 1.3 %gather_fusion = s32[128]{0:T(128)S(1)} fusion(s32[256]{0:T(256)S(1)} %copy-done.1, s32[1024]{0:T(1024)S(1)} %pad_clamp_fusion), kind=kCustom, calls=%fused_computation | custom fusion | bytes 1536 | tf_op jit(solution)/shard_map/gather | solution.py:98
  29.4 1.6 %collective-permute-start.1 = (bf16[1,64,512]{2,1,0:T(8,128)(2,1)S(1)}, bf16[1,64,512]{2,1,0:T(8,128)(2,1)S(1)}, u32[]{:S(2)}, u32[]{:S(2)}) collective-permute-start(bf16[1,64,512]{2,1,0:T(8,128)(2,1)S(1)} %collective-permute-done), channel_id=1, source_target_pairs={{0,1},{1,2},{2,3},{3,0},{4,5},{5,6},{6,7},{7,4},{8,9},{9,10},{10,1... | collective-permute-start | bytes 196616 | tf_op jit(solution)/shard_map/ppermute | solution.py:111
  31.1 1.3 %dynamic_slice.32 = s32[1]{0:T(128)} dynamic-slice(s32[4]{0:T(128)} %copy-done.11, s32[]{:T(128)S(6)} %select_n.62), dynamic_slice_sizes={1} | dynamic-slice | bytes 12 | tf_op jit(solution)/shard_map/dynamic_slice | solution.py:97
  32.4 10.2 %all-gather.1 = f32[4,1,16]{2,1,0:T(1,128)S(1)} all-gather(f32[1,1,16]{2,1,0:T(1,128)S(1)} %bitcast.82), channel_id=1, replica_groups=mesh['grp'=8,'seq'=4] {'seq'}, dimensions={0}, use_global_device_ids=true | all-gather | bytes 320 | tf_op jit(solution)/shard_map/all_gather | solution.py:9
  42.6 0.7 iota_compare_fusion.3
  43.3 6.9 %collective-permute-done.2 = bf16[1,64,512]{2,1,0:T(8,128)(2,1)S(1)} collective-permute-done((bf16[1,64,512]{2,1,0:T(8,128)(2,1)S(1)}, bf16[1,64,512]{2,1,0:T(8,128)(2,1)S(1)}, u32[]{:S(2)}, u32[]{:S(2)}) %collective-permute-start.2) | collective-permute-done | bytes 65568 | tf_op jit(solution)/shard_map/ppermute | solution.py:111
  55.1 10.3 %all-gather.4.cloned.1.call-done = f32[64,64,64]{2,1,0:T(8,128)} async-done(((f32[16,64,64]{2,1,0:T(8,128)}), f32[64,64,64]{2,1,0:T(8,128)}) %all-gather.4.cloned.1.call-update) | async-done | bytes 1048592 | tf_op jit(solution)/shard_map/all_gather | solution.py:9
  65.4 3.6 %while.18 = (s32[]{:T(128)}, f32[16,64,64]{2,1,0:T(8,128)S(1)}, s32[]{:T(128)}, f32[4,16]{1,0:T(4,128)S(1)}, f32[4,16,64,64]{3,2,1,0:T(8,128)}, /*index=5*/s32[]{:T(128)}, s32[]{:T(128)}) while((s32[]{:T(128)}, f32[16,64,64]{2,1,0:T(8,128)S(1)}, s32[]{:T(128)}, f32[4,16]{1,0:T(4,128)S(1)}, f32[4,16,64,64]{3,2,1,0:T(8,128)}, ...), condition=%wide.region_3.4_spmd.clone, body=%wide.region_2.3_spmd.clone.sunk | while | flops 262148 | bytes 786729 | solution.py:18
  65.4 1.2 %fusion.68 = f32[16,64,64]{2,1,0:T(8,128)S(1)} fusion(f32[4,16,64,64]{3,2,1,0:T(8,128)} %get-tuple-element.217, s32[]{:T(128)} %get-tuple-element.206, f32[16,64,64]{2,1,0:T(8,128)S(1)} %get-tuple-element.207, f32[16]{0:T(128)S(1)} %dynamic-slice_bitcast_fusion.2, pred[]{:T(512)S(6)} %compare.4, pred[]{:T(512)S(6)} %lt.134), kind=kLoop, calls=%fused_computation.2.clone.1 | loop fusion | flops 262144 | bytes 786502 | tf_op jit(solution)/shard_map/while/body/eval_jaxpr/jit(_where)/select_n | solution.py:16
  66.6 1.2 %fusion.68 = f32[16,64,64]{2,1,0:T(8,128)S(1)} fusion(f32[4,16,64,64]{3,2,1,0:T(8,128)} %get-tuple-element.217, s32[]{:T(128)} %get-tuple-element.206, f32[16,64,64]{2,1,0:T(8,128)S(1)} %get-tuple-element.207, f32[16]{0:T(128)S(1)} %dynamic-slice_bitcast_fusion.2, pred[]{:T(512)S(6)} %compare.4, pred[]{:T(512)S(6)} %lt.134), kind=kLoop, calls=%fused_computation.2.clone.1 | loop fusion | flops 262144 | bytes 786502 | tf_op jit(solution)/shard_map/while/body/eval_jaxpr/jit(_where)/select_n | solution.py:16
  67.9 1.2 %fusion.68 = f32[16,64,64]{2,1,0:T(8,128)S(1)} fusion(f32[4,16,64,64]{3,2,1,0:T(8,128)} %get-tuple-element.217, s32[]{:T(128)} %get-tuple-element.206, f32[16,64,64]{2,1,0:T(8,128)S(1)} %get-tuple-element.207, f32[16]{0:T(128)S(1)} %dynamic-slice_bitcast_fusion.2, pred[]{:T(512)S(6)} %compare.4, pred[]{:T(512)S(6)} %lt.134), kind=kLoop, calls=%fused_computation.2.clone.1 | loop fusion | flops 262144 | bytes 786502 | tf_op jit(solution)/shard_map/while/body/eval_jaxpr/jit(_where)/select_n | solution.py:16
  69.1 2.4 %fusion.15 = f32[256,16,64]{0,2,1:T(8,128)S(1)} fusion(f32[256,16,64]{0,2,1:T(8,128)} %fusion.11, f32[16,64,64]{2,1,0:T(8,128)S(1)} %get-tuple-element.123, f32[256,16]{0,1:T(8,128)S(1)} %copy-done.8, f32[256,64]{0,1:T(8,128)S(1)} %slice_convert_fusion), kind=kOutput, calls=%fused_computation.19 | convolution fusion | flops 201850880 | bytes 2441216 | tf_op jit(solution)/shard_map/ih,in,hpn->ihp/dot_general | solution.py:81
  71.5 1.4 %multiply_reduce_fusion = (f32[256]{0:T(256)S(1)}, f32[256,1024]{0,1:T(8,128)S(1)}) fusion(bf16[256,2176]{0,1:T(8,128)(2,1)} %copy-done.2, f32[256,16,64]{0,2,1:T(8,128)S(1)} %fusion.15), kind=kLoop, calls=%fused_computation.36 | loop fusion | flops 2096896 | bytes 2622464 | tf_op jit(solution)/shard_map/reduce_sum | solution.py:22
  73.0 0.8 fusion.16
  74.2 15.6 %all_gather.16 = bf16[512,512]{1,0:T(8,128)(2,1)S(1)} all-gather(bf16[128,512]{1,0:T(8,128)(2,1)S(1)} %multiply_convert_fusion.2), channel_id=1, replica_groups=mesh['grp'=8,'seq'=4] {'seq'}, dimensions={0}, use_global_device_ids=true | all-gather | bytes 655360 | tf_op jit(solution)/shard_map/all_gather | solution.py:104
  91.6 0.7 reduce.6
  92.4 0.8 reshape.183
  93.2 3.3 %all-to-all-start = ((bf16[4,2,4096]{2,1,0:T(2,128)(2,1)}), bf16[4,2,4096]{2,1,0:T(2,128)(2,1)S(1)}, u32[]{:S(2)}, u32[]{:S(2)}) async-start(bf16[4,2,4096]{2,1,0:T(2,128)(2,1)} %reshape.183), calls=%async_computation | async-start | bytes 131072 | tf_op jit(solution)/shard_map/all_to_all | solution.py:115
  96.5 1.0 constant_dynamic-slice_fusion
  97.5 4.7 %all-to-all-done = bf16[4,2,4096]{2,1,0:T(2,128)(2,1)S(1)} async-done(((bf16[4,2,4096]{2,1,0:T(2,128)(2,1)}), bf16[4,2,4096]{2,1,0:T(2,128)(2,1)S(1)}, u32[]{:S(2)}, u32[]{:S(2)}) %all-to-all-start) | async-done | bytes 65568 | tf_op jit(solution)/shard_map/all_to_all | solution.py:115
  102.7 1.2 %fusion.17 = bf16[256,512]{1,0:T(8,128)(2,1)} fusion(f32[128,512]{1,0:T(8,128)S(1)} %fusion.55, bf16[256,512]{1,0:T(8,128)(2,1)S(1)} %fusion.16, s32[128]{0:T(128)S(1)} %broadcast_subtract_fusion, pred[128]{0:T(512)(128)(4,1)S(1)} %iota_compare_fusion.3), kind=kOutput, calls=%fused_computation.25 | convolution fusion | flops 201785344 | bytes 787072 | tf_op jit(solution)/shard_map/dot_general | solution.py:121
  (70 shorter events, 11.5 us)
Async XLA Ops:
  6.5 3.2 %copy-start = (bf16[512,2176]{1,0:T(8,128)(2,1)S(1)}, bf16[512,2176]{1,0:T(8,128)(2,1)}, u32[]{:S(2)}) copy-start(bf16[512,2176]{1,0:T(8,128)(2,1)} %param.14) | copy-start | bytes 6684676
  6.5 58.9 %all-gather.4.cloned.1.call-start = ((), (), s32[]{:S(2)}) async-start(), calls=%async_computation.1 | async-start | bytes 2621440 | tf_op jit(solution)/shard_map/all_gather | solution.py:9
  11.7 16.4 %copy-start.2 = (bf16[256,2176]{0,1:T(8,128)(2,1)}, bf16[256,2176]{0,1:T(8,128)(2,1)S(1)}, u32[]{:S(2)}) copy-start(bf16[256,2176]{0,1:T(8,128)(2,1)S(1)} %convolution_convert_fusion) | copy-start | bytes 3342340
  11.7 2.4 %copy-start.6 = (bf16[1,64,512]{2,1,0:T(8,128)(2,1)S(1)}, bf16[1,64,512]{2,1,0:T(8,128)(2,1)}, u32[]{:S(2)}) copy-start(bf16[1,64,512]{2,1,0:T(8,128)(2,1)} %param.19) | copy-start | bytes 196612
  11.7 7.6 %copy-start.1 = (s32[256]{0:T(256)S(1)}, s32[256]{0:T(256)}, u32[]{:S(2)}) copy-start(s32[256]{0:T(256)} %param.12) | copy-start | bytes 3076
  11.8 0.8 copy-start.3
  14.1 15.4 %collective-permute-start = (bf16[1,64,512]{2,1,0:T(8,128)(2,1)S(1)}, bf16[1,64,512]{2,1,0:T(8,128)(2,1)S(1)}, u32[]{:S(2)}, u32[]{:S(2)}) collective-permute-start(bf16[1,64,512]{2,1,0:T(8,128)(2,1)S(1)} %copy-done.6), channel_id=1, source_target_pairs={{0,1},{1,2},{2,3},{3,0},{4,5},{5,6},{6,7},{7,4},{8,9},{9,10},{10,1... | collective-permute-start | bytes 196616 | tf_op jit(solution)/shard_map/ppermute | solution.py:111
  22.6 5.5 %copy-start.11 = (s32[4]{0:T(128)}, s32[4]{0:T(128)S(1)}, u32[]{:S(2)}) copy-start(s32[4]{0:T(128)S(1)} %sub.64) | copy-start | bytes 52
  29.4 13.1 %collective-permute-start.1 = (bf16[1,64,512]{2,1,0:T(8,128)(2,1)S(1)}, bf16[1,64,512]{2,1,0:T(8,128)(2,1)S(1)}, u32[]{:S(2)}, u32[]{:S(2)}) collective-permute-start(bf16[1,64,512]{2,1,0:T(8,128)(2,1)S(1)} %collective-permute-done), channel_id=1, source_target_pairs={{0,1},{1,2},{2,3},{3,0},{4,5},{5,6},{6,7},{7,4},{8,9},{9,10},{10,1... | collective-permute-start | bytes 196616 | tf_op jit(solution)/shard_map/ppermute | solution.py:111
  42.6 7.6 %collective-permute-start.2 = (bf16[1,64,512]{2,1,0:T(8,128)(2,1)S(1)}, bf16[1,64,512]{2,1,0:T(8,128)(2,1)S(1)}, u32[]{:S(2)}, u32[]{:S(2)}) collective-permute-start(bf16[1,64,512]{2,1,0:T(8,128)(2,1)S(1)} %collective-permute-done.1), channel_id=1, source_target_pairs={{0,1},{1,2},{2,3},{3,0},{4,5},{5,6},{6,7},{7,4},{8,9},{9,10},{10,1... | collective-permute-start | bytes 196616 | tf_op jit(solution)/shard_map/ppermute | solution.py:111
  65.4 3.6 %copy-start.8 = (f32[256,16]{0,1:T(8,128)S(1)}, f32[256,16]{0,1:T(8,128)}, u32[]{:S(2)}) copy-start(f32[256,16]{0,1:T(8,128)} %get-tuple-element.158) | copy-start | bytes 49156
  69.1 3.9 %copy-start.4 = (bf16[256,512]{1,0:T(8,128)(2,1)S(1)}, bf16[256,512]{1,0:T(8,128)(2,1)}, u32[]{:S(2)}) copy-start(bf16[256,512]{1,0:T(8,128)(2,1)} %param.11) | copy-start | bytes 786436
  69.1 3.9 %copy-start.5 = (bf16[1024,512]{1,0:T(8,128)(2,1)S(1)}, bf16[1024,512]{1,0:T(8,128)(2,1)}, u32[]{:S(2)}) copy-start(bf16[1024,512]{1,0:T(8,128)(2,1)} %param.16) | copy-start | bytes 3145732
  69.1 3.9 %copy-start.9 = (f32[1024]{0:T(1024)S(1)}, f32[1024]{0:T(1024)}, u32[]{:S(2)}) copy-start(f32[1024]{0:T(1024)} %param.15) | copy-start | bytes 12292
  72.9 1.2 %copy-start.10 = (f32[512]{0:T(512)S(1)}, f32[512]{0:T(512)}, u32[]{:S(2)}) copy-start(f32[512]{0:T(512)} %param.17) | copy-start | bytes 6148
  72.9 16.9 %copy-start.7 = (bf16[1,512,192]{1,2,0:T(8,128)(2,1)S(1)}, bf16[1,512,192]{1,2,0:T(8,128)(2,1)}, u32[]{:S(2)}) copy-start(bf16[1,512,192]{1,2,0:T(8,128)(2,1)} %param.18) | copy-start | bytes 589828
  93.2 9.0 %all-to-all-start = ((bf16[4,2,4096]{2,1,0:T(2,128)(2,1)}), bf16[4,2,4096]{2,1,0:T(2,128)(2,1)S(1)}, u32[]{:S(2)}, u32[]{:S(2)}) async-start(bf16[4,2,4096]{2,1,0:T(2,128)(2,1)} %reshape.183), calls=%async_computation | async-start | bytes 131072 | tf_op jit(solution)/shard_map/all_to_all | solution.py:115
Sparse Core Ops, SparseCore 0:
  14.2 51.2 all-gather.3
